TPU v7x, 256 devices: a whole 4x4x8 slice. The times are simulated.
256 devices in a mesh: ctx: 16 (over y, x), exp: 16 (over z, core).
Axes of the slice: x: 4, y: 4, z: 8, core: 2. Of those that a mesh axis runs over, the one named last changes fastest.
Arguments:
- tokens: bfloat16 [2048, 4096], P('ctx', 'exp'), may hold values from -6 to 6
- input_weight: bfloat16 [4096, 8192], P('ctx', 'exp'), may hold values from -0.09375 to 0.09375
- gate_weight: bfloat16 [4096, 8192], P('ctx', 'exp'), may hold values from -0.09375 to 0.09375
- conv_weight: float32 [4, 8192], P(None, 'exp'), may hold values from -3 to 3
- conv_bias: float32 [8192], P('exp'), may hold values from -3 to 3
- state_weight: bfloat16 [8192, 32], P('exp'), may hold values from -0.0078125 to 0.0078125
- step_size: float32 [2048, 8192], P('ctx', 'exp'), may hold values from 0 to 1, as said below
- skip_gain: float32 [8192], P('exp'), may hold values from 0.5 to 2
- output_weight: bfloat16 [8192, 4096], P('exp', 'ctx'), may hold values from -0.0625 to 0.0625
- norm_gain: float32 [4096], replicated, may hold values from 0.1 to 1.9
- router_weight: bfloat16 [4096, 16], replicated, may hold values from -0.09375 to 0.09375
- expert_gate: bfloat16 [16, 7168, 4096], P('exp', 'ctx'), may hold values from -0.09375 to 0.09375
- expert_up: bfloat16 [16, 7168, 4096], P('exp', 'ctx'), may hold values from -0.09375 to 0.09375
- expert_down: bfloat16 [16, 7168, 4096], P('exp', 'ctx'), may hold values from -0.0625 to 0.0625
- expert_ids: int32 [2048, 2], P(('ctx', 'exp')), may hold values from 0 to 15, all different within a row; in each aligned block of 8 rows (0 to 7, 8 to 15, ...) at most 2 rows name the same one
Outputs:
- layer_out: bfloat16 [2048, 4096], P(('ctx', 'exp'))
Inputs may be any that keep to these rules, and one draw needn't show every extreme that they name: `expert_ids`: each token names 2 different experts; in each aligned block of 8 tokens no expert is named by more than 2 tokens. `step_size`: a positive rate for each token and channel.
All inputs are finite; a program needn't handle non-finite values.
Results may differ from a plain program's by a relative error of at most 0.028.
Values may be sent and summed in bfloat16 or wider, within the bound.
A program may use at most 128 MiB of HBM per device.

v0:
```python
import jax
import jax.numpy as jnp
from jax import lax
from jax.sharding import PartitionSpec as P

STATE = 16
CONV = 4
TOP = 2
CAP = 2
precise = lax.Precision.HIGHEST


def shifted(shard, axis, by):
    devices = lax.axis_size(axis)
    pairs = [(i, i + by) for i in range(devices) if 0 <= i + by < devices]
    return lax.ppermute(shard, axis, pairs)


def causal_part(scores, decay_block, input_block):
    length = decay_block.shape[0]
    causal = (jnp.arange(length)[:, None] >= jnp.arange(length)[None, :])[:, :, None]
    distance = decay_block[:, None, :] - decay_block[None, :, :]
    weight = jnp.where(causal, jnp.exp(-jnp.where(causal, distance, 0.0)), 0.0)
    return jnp.einsum("ts,tsc,sc->tc", scores, weight, input_block, precision=precise)


def local(
    tokens,
    input_weight,
    gate_weight,
    conv_weight,
    conv_bias,
    state_weight,
    step_size,
    skip_gain,
    output_weight,
    norm_gain,
    router_weight,
    expert_gate,
    expert_up,
    expert_down,
    expert_ids,
):
    whole_stretch = lax.all_gather(tokens, "exp", axis=1, tiled=True)
    stretch_rows = whole_stretch.shape[0]
    inner_width = input_weight.shape[1]
    inner_x = jnp.dot(
        whole_stretch,
        lax.all_gather(input_weight, "ctx", axis=0, tiled=True),
        preferred_element_type=jnp.float32,
    )
    inner_z = jnp.dot(
        whole_stretch,
        lax.all_gather(gate_weight, "ctx", axis=0, tiled=True),
        preferred_element_type=jnp.float32,
    )
    inner_x = inner_x.astype(jnp.bfloat16)
    inner_z = inner_z.astype(jnp.bfloat16)
    earlier_rows = shifted(inner_x[stretch_rows - (CONV - 1) :], "ctx", 1)
    extended = jnp.concatenate([earlier_rows, inner_x], 0).astype(jnp.float32)
    filtered = jnp.broadcast_to(conv_bias[None, :], (stretch_rows, inner_width))
    for offset in range(CONV):
        filtered = (
            filtered + conv_weight[offset][None, :] * extended[offset : offset + stretch_rows]
        )
    mixer_in = jax.nn.silu(filtered).astype(jnp.bfloat16)
    mixer_wide = mixer_in.astype(jnp.float32)
    projections = lax.psum(
        jnp.dot(mixer_in, state_weight, preferred_element_type=jnp.float32), "exp"
    )
    input_gain = projections[:, :STATE]
    readout = projections[:, STATE:]
    cumulative = jnp.cumsum(step_size, 0)
    scores = jnp.dot(readout, input_gain.T, precision=precise)
    block_width = 128
    block_count = inner_width // block_width
    decay_blocks = cumulative.reshape(stretch_rows, block_count, block_width).transpose(1, 0, 2)
    incoming_slabs = mixer_wide.reshape(stretch_rows, block_count, block_width).transpose(1, 0, 2)
    inside = lax.map(
        lambda paired: causal_part(scores, paired[0], paired[1]), (decay_blocks, incoming_slabs)
    )
    inside = inside.transpose(1, 0, 2).reshape(stretch_rows, inner_width)
    total_decay = cumulative[stretch_rows - 1]
    tail_weight = jnp.exp(-(total_decay[None, :] - cumulative)) * mixer_wide
    local_end = jnp.dot(tail_weight.T, input_gain, precision=precise)
    stretch_keep = jnp.exp(-total_decay)

    def relay_step(turn_index, received):
        leaving = stretch_keep[:, None] * received + local_end
        return shifted(leaving, "ctx", 1)

    entering = lax.fori_loop(0, lax.axis_size("ctx") - 1, relay_step, jnp.zeros_like(local_end))
    carried = jnp.exp(-cumulative) * jnp.dot(readout, entering.T, precision=precise)
    mixed_state = (inside + carried + skip_gain[None, :] * mixer_wide) * jax.nn.silu(
        inner_z.astype(jnp.float32)
    )
    blender_result = mixed_state.astype(jnp.bfloat16)
    row_count = expert_ids.shape[0]
    start_row = lax.axis_index("exp") * row_count
    own_tokens = lax.dynamic_slice_in_dim(whole_stretch, start_row, row_count, 0)
    out_whole = lax.all_gather(output_weight, "ctx", axis=1, tiled=True)
    projected = lax.psum_scatter(
        jnp.dot(blender_result, out_whole, preferred_element_type=jnp.float32).astype(jnp.bfloat16),
        "exp",
        scatter_dimension=0,
        tiled=True,
    ).astype(jnp.float32)
    residual = (own_tokens.astype(jnp.float32) + projected).astype(jnp.bfloat16)
    stream = residual.astype(jnp.float32)
    normed = (
        stream
        * lax.rsqrt(jnp.mean(stream * stream, -1, keepdims=True) + 1e-05)
        * norm_gain[None, :]
    ).astype(jnp.bfloat16)
    logits = jnp.dot(normed, router_weight, preferred_element_type=jnp.float32)
    experts = router_weight.shape[1]
    expert_range = jnp.arange(experts, dtype=jnp.int32)
    chosen = expert_ids[:, :, None] == expert_range[None, None, :]
    selected_entry = jnp.sum(jnp.where(chosen, logits[:, None, :], 0.0), -1)
    shares = jax.nn.sigmoid(selected_entry - selected_entry[:, ::-1])
    flat_hits = chosen.reshape(row_count * TOP, experts).astype(jnp.int32)
    earlier_hits = jnp.cumsum(flat_hits, 0) - flat_hits
    slot_index = jnp.sum(earlier_hits * flat_hits, -1)
    target = expert_ids.reshape(-1) * CAP + slot_index
    placed = target[:, None] == jnp.arange(experts * CAP, dtype=jnp.int32)[None, :]
    placed = placed.reshape(row_count, TOP, experts * CAP)
    selector = jnp.any(placed, 1).astype(jnp.bfloat16)
    outgoing = lax.dot_general(
        selector, normed, (((0,), (0,)), ((), ())), preferred_element_type=jnp.float32
    ).astype(jnp.bfloat16)
    outgoing = outgoing.reshape(experts, CAP, -1)
    arrived = lax.all_to_all(outgoing, "exp", split_axis=0, concat_axis=0, tiled=True)
    arrived = arrived.reshape(-1, arrived.shape[2])
    gate_part = expert_gate[0]
    up_part = expert_up[0]
    down_part = expert_down[0]
    shard_rows = lax.all_gather(arrived, "ctx", axis=0, tiled=True)
    gate_value = lax.dot_general(
        shard_rows, gate_part, (((1,), (1,)), ((), ())), preferred_element_type=jnp.float32
    )
    up_value = lax.dot_general(
        shard_rows, up_part, (((1,), (1,)), ((), ())), preferred_element_type=jnp.float32
    )
    hidden = (jax.nn.silu(gate_value) * up_value).astype(jnp.bfloat16)
    partial_out = jnp.dot(hidden, down_part, preferred_element_type=jnp.float32)
    finished = lax.psum_scatter(
        partial_out.astype(jnp.bfloat16), "ctx", scatter_dimension=0, tiled=True
    )
    returned = lax.all_to_all(
        finished.reshape(experts, CAP, -1), "exp", split_axis=0, concat_axis=0, tiled=True
    )
    returned = returned.reshape(experts * CAP, -1).astype(jnp.float32)
    combine = jnp.sum(jnp.where(placed, shares[:, :, None], 0.0), 1)
    moe_out = jnp.dot(combine, returned, precision=precise)
    return (stream + moe_out).astype(jnp.bfloat16)


def solution(mesh):
    in_specs = (
        P("ctx", "exp"),
        P("ctx", "exp"),
        P("ctx", "exp"),
        P(None, "exp"),
        P("exp"),
        P("exp", None),
        P("ctx", "exp"),
        P("exp"),
        P("exp", "ctx"),
        P(),
        P(),
        P("exp", "ctx", None),
        P("exp", "ctx", None),
        P("exp", "ctx", None),
        P(("ctx", "exp"), None),
    )
    out_specs = P(("ctx", "exp"), None)
    return jax.shard_map(local, mesh=mesh, in_specs=in_specs, out_specs=out_specs, check_vma=False)
```

profile of v0, /device:TPU:1, one launch (start us, length us, event | category | flops | bytes accessed | tf_op | source)
XLA Modules:
  0.0 636.4 jit_solution(2759990935749958650)
XLA Ops:
  11.5 39.5 %all-gather.6.cloned.1.call-done = bf16[128,4096]{1,0:T(8,128)(2,1)} async-done(((bf16[128,256]{1,0:T(8,128)(2,1)}), bf16[128,4096]{1,0:T(8,128)(2,1)}) %all-gather.6.cloned.1.call-update) | async-done | bytes 1048592 | tf_op jit(solution)/shard_map/all_gather | solution.py:44
  51.0 57.7 %all-gather.8.cloned.1.call-done = bf16[4096,512]{1,0:T(8,128)(2,1)} async-done(((bf16[256,512]{1,0:T(8,128)(2,1)}), bf16[4096,512]{1,0:T(8,128)(2,1)}) %all-gather.8.cloned.1.call-update) | async-done | bytes 4194320 | tf_op jit(solution)/shard_map/all_gather | solution.py:49
  115.1 52.4 %all-gather.10.cloned.1.call-done = bf16[4096,512]{1,0:T(8,128)(2,1)} async-done(((bf16[256,512]{1,0:T(8,128)(2,1)}), bf16[4096,512]{1,0:T(8,128)(2,1)}) %all-gather.10.cloned.1.call-update) | async-done | bytes 4194320 | tf_op jit(solution)/shard_map/all_gather | solution.py:54
  170.7 46.7 %psum.7 = f32[128,32]{0,1:T(8,128)S(1)} all-reduce(f32[128,32]{0,1:T(8,128)S(1)} %fusion.54), channel_id=1, replica_groups=mesh['ctx'=16,'exp'=16] {'exp'}, use_global_device_ids=true, to_apply=%region_1.2 | all-reduce | flops 4096 | bytes 32768 | tf_op jit(solution)/shard_map/psum | solution.py:68
  218.1 39.1 %while.20 = (s32[]{:T(128)}, f32[4,128,128]{2,1,0:T(8,128)S(1)}, f32[4,128,128]{2,1,0:T(8,128)S(1)}, f32[4,128,128]{2,1,0:T(8,128)S(1)}, f32[128,128]{1,0:T(8,128)S(1)}, /*index=5*/s32[]{:T(128)}) while((s32[]{:T(128)}, f32[4,128,128]{2,1,0:T(8,128)S(1)}, f32[4,128,128]{2,1,0:T(8,128)S(1)}, f32[4,128,128]{2,1,0:T(8,128)S(1)}, ...), condition=%wide.region_3.4_spmd, body=%wide.region_2.3_spmd.sunk | while | flops 35667968 | bytes 688205 | solution.py:79
  218.1 9.7 %fusion.87 = f32[128,1,128]{2,1,0:T(1,128)S(1)} fusion(f32[128,128,1]{1,2,0:T(1,128)S(1)} %bitcast.88, f32[128,128]{1,0:T(8,128)S(1)} %get-tuple-element.140, f32[128,128]{1,0:T(8,128)S(1)} %get-tuple-element.141, pred[128,128]{1,0:T(8,128)(4,1)S(1)} %iota_compare_fusion.5), kind=kOutput, calls=%fused_computation.clone.1 | convolution fusion | flops 35651584 | bytes 278528 | tf_op jit(solution)/shard_map/while/body/eval_jaxpr/ts,tsc,sc->tc/dot_general | solution.py:24
  227.9 9.7 %fusion.87 = f32[128,1,128]{2,1,0:T(1,128)S(1)} fusion(f32[128,128,1]{1,2,0:T(1,128)S(1)} %bitcast.88, f32[128,128]{1,0:T(8,128)S(1)} %get-tuple-element.140, f32[128,128]{1,0:T(8,128)S(1)} %get-tuple-element.141, pred[128,128]{1,0:T(8,128)(4,1)S(1)} %iota_compare_fusion.5), kind=kOutput, calls=%fused_computation.clone.1 | convolution fusion | flops 35651584 | bytes 278528 | tf_op jit(solution)/shard_map/while/body/eval_jaxpr/ts,tsc,sc->tc/dot_general | solution.py:24
  237.6 9.7 %fusion.87 = f32[128,1,128]{2,1,0:T(1,128)S(1)} fusion(f32[128,128,1]{1,2,0:T(1,128)S(1)} %bitcast.88, f32[128,128]{1,0:T(8,128)S(1)} %get-tuple-element.140, f32[128,128]{1,0:T(8,128)S(1)} %get-tuple-element.141, pred[128,128]{1,0:T(8,128)(4,1)S(1)} %iota_compare_fusion.5), kind=kOutput, calls=%fused_computation.clone.1 | convolution fusion | flops 35651584 | bytes 278528 | tf_op jit(solution)/shard_map/while/body/eval_jaxpr/ts,tsc,sc->tc/dot_general | solution.py:24
  247.4 9.7 %fusion.87 = f32[128,1,128]{2,1,0:T(1,128)S(1)} fusion(f32[128,128,1]{1,2,0:T(1,128)S(1)} %bitcast.88, f32[128,128]{1,0:T(8,128)S(1)} %get-tuple-element.140, f32[128,128]{1,0:T(8,128)S(1)} %get-tuple-element.141, pred[128,128]{1,0:T(8,128)(4,1)S(1)} %iota_compare_fusion.5), kind=kOutput, calls=%fused_computation.clone.1 | convolution fusion | flops 35651584 | bytes 278528 | tf_op jit(solution)/shard_map/while/body/eval_jaxpr/ts,tsc,sc->tc/dot_general | solution.py:24
  257.1 90.6 %while.21 = (s32[]{:T(128)}, f32[512,16]{0,1:T(8,128)S(1)}, f32[512]{0:T(512)S(1)}, f32[512,16]{0,1:T(8,128)S(1)}, s32[]{:T(128)}) while((s32[]{:T(128)}, f32[512,16]{0,1:T(8,128)S(1)}, f32[512]{0:T(512)S(1)}, f32[512,16]{0,1:T(8,128)S(1)}, s32[]{:T(128)}) %tuple.40), condition=%wide.region_5.6_spmd, body=%wide.region_4.5_spmd.sunk | while | flops 16386 | bytes 231525 | solution.py:92
  280.0 5.8 collective-permute-start
  293.5 5.8 collective-permute-start
  300.3 5.8 collective-permute-start
  307.1 5.8 collective-permute-start
  313.8 5.8 collective-permute-start
  320.6 5.8 collective-permute-start
  340.9 5.8 collective-permute-start
  352.9 81.0 %reduce-scatter.3.cloned.1.call-done = bf16[8,4096]{1,0:T(8,128)(2,1)} async-done(((bf16[128,4096]{1,0:T(8,128)(2,1)}), bf16[8,4096]{1,0:T(8,128)(2,1)}) %reduce-scatter.3.cloned.1.call-update) | async-done | bytes 65552 | tf_op jit(solution)/shard_map/reduce_scatter | solution.py:102
  435.4 19.1 %all_to_all.10 = bf16[16,2,4096]{2,1,0:T(2,128)(2,1)S(1)} all-to-all(bf16[16,2,4096]{2,1,0:T(2,128)(2,1)S(1)} %reshape.74), channel_id=1, replica_groups=mesh['ctx'=16,'exp'=16] {'exp'}, dimensions={0} | all-to-all | bytes 524288 | tf_op jit(solution)/shard_map/all_to_all | solution.py:132
  455.5 53.0 %all-gather.14.cloned.1.call-done = bf16[512,4096]{1,0:T(8,128)(2,1)} async-done(((bf16[32,4096]{1,0:T(8,128)(2,1)}), bf16[512,4096]{1,0:T(8,128)(2,1)}) %all-gather.14.cloned.1.call-update) | async-done | bytes 4194320 | tf_op jit(solution)/shard_map/all_gather | solution.py:137
  513.9 10.8 %convolution_convert_fusion = bf16[512,4096]{1,0:T(8,128)(2,1)} fusion(bf16[1,448,4096]{2,1,0:T(8,128)(2,1)} %param.32, bf16[512,4096]{1,0:T(8,128)(2,1)} %all-gather.14.cloned.1.call-done, bf16[1,448,4096]{2,1,0:T(8,128)(2,1)} %param.31, f32[512,448]{0,1:T(8,128)S(1)} %fusion.18), kind=kOutput, calls=%fused_computation.19 | convolution fusion | flops 3761569792 | bytes 16646144 | tf_op jit(solution)/shard_map/dot_general | solution.py:145
  524.7 81.0 %reduce-scatter.5.cloned.1.call-done = bf16[32,4096]{1,0:T(8,128)(2,1)} async-done(((bf16[512,4096]{1,0:T(8,128)(2,1)}), bf16[32,4096]{1,0:T(8,128)(2,1)}) %reduce-scatter.5.cloned.1.call-update) | async-done | bytes 262160 | tf_op jit(solution)/shard_map/reduce_scatter | solution.py:146
  607.5 9.3 %all-to-all-start.1 = ((bf16[16,2,4096]{2,1,0:T(2,128)(2,1)}), bf16[16,2,4096]{2,1,0:T(2,128)(2,1)S(1)}, u32[]{:S(2)}, u32[]{:S(2)}) async-start(bf16[16,2,4096]{2,1,0:T(2,128)(2,1)} %reshape.76), calls=%async_computation.3 | async-start | bytes 524288 | tf_op jit(solution)/shard_map/all_to_all | solution.py:149
  617.3 11.2 %all-to-all-done.1 = bf16[16,2,4096]{2,1,0:T(2,128)(2,1)S(1)} async-done(((bf16[16,2,4096]{2,1,0:T(2,128)(2,1)}), bf16[16,2,4096]{2,1,0:T(2,128)(2,1)S(1)}, u32[]{:S(2)}, u32[]{:S(2)}) %all-to-all-start.1) | async-done | bytes 262176 | tf_op jit(solution)/shard_map/all_to_all | solution.py:149
  (121 shorter events, 81.6 us)
Async XLA Ops:
  6.5 44.5 %all-gather.6.cloned.1.call-start = ((), (), s32[]{:S(2)}) async-start(), calls=%async_computation.4 | async-start | bytes 1114112 | tf_op jit(solution)/shard_map/all_gather | solution.py:44
  7.3 101.4 %all-gather.8.cloned.1.call-start = ((), (), s32[]{:S(2)}) async-start(), calls=%async_computation.5 | async-start | bytes 4456448 | tf_op jit(solution)/shard_map/all_gather | solution.py:49
  8.0 159.4 %all-gather.10.cloned.1.call-start = ((), (), s32[]{:S(2)}) async-start(), calls=%async_computation.6 | async-start | bytes 4456448 | tf_op jit(solution)/shard_map/all_gather | solution.py:54
  8.7 339.5 %all-gather.12.cloned.1.call-start = ((), (), s32[]{:S(2)}) async-start(), calls=%async_computation.7 | async-start | bytes 4456448 | tf_op jit(solution)/shard_map/all_gather | solution.py:101
  9.3 424.6 %reduce-scatter.3.cloned.1.call-start = ((), (), s32[]{:S(2)}) async-start(), calls=%async_computation.8 | async-start | bytes 1114112 | tf_op jit(solution)/shard_map/reduce_scatter | solution.py:102
  112.0 58.4 %collective-permute-start.1 = (bf16[3,512]{1,0:T(4,128)(2,1)S(1)}, bf16[3,512]{1,0:T(4,128)(2,1)S(1)}, u32[]{:S(2)}, u32[]{:S(2)}) collective-permute-start(bf16[3,512]{1,0:T(4,128)(2,1)S(1)} %slice.48), channel_id=1, source_target_pairs={{0,16},{16,32},{32,48},{48,64},{64,80},{80,96},{96,112},{112,128},... | collective-permute-start | bytes 9224 | tf_op jit(solution)/shard_map/ppermute | solution.py:16
  257.2 3.7 collective-permute-start
  260.9 4.7 collective-permute-start
  265.5 4.7 collective-permute-start
  270.2 5.1 collective-permute-start
  275.3 4.7 collective-permute-start
  280.0 6.9 %collective-permute-start = (f32[512,16]{0,1:T(8,128)S(1)}, f32[512,16]{0,1:T(8,128)S(1)}, u32[]{:S(2)}, u32[]{:S(2)}) collective-permute-start(f32[512,16]{0,1:T(8,128)S(1)} %multiply_add_fusion.3), channel_id=1, source_target_pairs={{0,16},{16,32},{32,48},{48,64},{64,80},{80,96},{96,112},{112,128},... | collective-permute-start | bytes 98312 | tf_op jit(solution)/shard_map/while/body/eval_jaxpr/ppermute | solution.py:16
  286.8 6.7 %collective-permute-start = (f32[512,16]{0,1:T(8,128)S(1)}, f32[512,16]{0,1:T(8,128)S(1)}, u32[]{:S(2)}, u32[]{:S(2)}) collective-permute-start(f32[512,16]{0,1:T(8,128)S(1)} %multiply_add_fusion.3), channel_id=1, source_target_pairs={{0,16},{16,32},{32,48},{48,64},{64,80},{80,96},{96,112},{112,128},... | collective-permute-start | bytes 98312 | tf_op jit(solution)/shard_map/while/body/eval_jaxpr/ppermute | solution.py:16
  293.5 6.8 %collective-permute-start = (f32[512,16]{0,1:T(8,128)S(1)}, f32[512,16]{0,1:T(8,128)S(1)}, u32[]{:S(2)}, u32[]{:S(2)}) collective-permute-start(f32[512,16]{0,1:T(8,128)S(1)} %multiply_add_fusion.3), channel_id=1, source_target_pairs={{0,16},{16,32},{32,48},{48,64},{64,80},{80,96},{96,112},{112,128},... | collective-permute-start | bytes 98312 | tf_op jit(solution)/shard_map/while/body/eval_jaxpr/ppermute | solution.py:16
  300.3 6.8 %collective-permute-start = (f32[512,16]{0,1:T(8,128)S(1)}, f32[512,16]{0,1:T(8,128)S(1)}, u32[]{:S(2)}, u32[]{:S(2)}) collective-permute-start(f32[512,16]{0,1:T(8,128)S(1)} %multiply_add_fusion.3), channel_id=1, source_target_pairs={{0,16},{16,32},{32,48},{48,64},{64,80},{80,96},{96,112},{112,128},... | collective-permute-start | bytes 98312 | tf_op jit(solution)/shard_map/while/body/eval_jaxpr/ppermute | solution.py:16
  307.1 6.8 %collective-permute-start = (f32[512,16]{0,1:T(8,128)S(1)}, f32[512,16]{0,1:T(8,128)S(1)}, u32[]{:S(2)}, u32[]{:S(2)}) collective-permute-start(f32[512,16]{0,1:T(8,128)S(1)} %multiply_add_fusion.3), channel_id=1, source_target_pairs={{0,16},{16,32},{32,48},{48,64},{64,80},{80,96},{96,112},{112,128},... | collective-permute-start | bytes 98312 | tf_op jit(solution)/shard_map/while/body/eval_jaxpr/ppermute | solution.py:16
  313.8 6.8 %collective-permute-start = (f32[512,16]{0,1:T(8,128)S(1)}, f32[512,16]{0,1:T(8,128)S(1)}, u32[]{:S(2)}, u32[]{:S(2)}) collective-permute-start(f32[512,16]{0,1:T(8,128)S(1)} %multiply_add_fusion.3), channel_id=1, source_target_pairs={{0,16},{16,32},{32,48},{48,64},{64,80},{80,96},{96,112},{112,128},... | collective-permute-start | bytes 98312 | tf_op jit(solution)/shard_map/while/body/eval_jaxpr/ppermute | solution.py:16
  320.6 6.9 %collective-permute-start = (f32[512,16]{0,1:T(8,128)S(1)}, f32[512,16]{0,1:T(8,128)S(1)}, u32[]{:S(2)}, u32[]{:S(2)}) collective-permute-start(f32[512,16]{0,1:T(8,128)S(1)} %multiply_add_fusion.3), channel_id=1, source_target_pairs={{0,16},{16,32},{32,48},{48,64},{64,80},{80,96},{96,112},{112,128},... | collective-permute-start | bytes 98312 | tf_op jit(solution)/shard_map/while/body/eval_jaxpr/ppermute | solution.py:16
  327.6 6.6 %collective-permute-start = (f32[512,16]{0,1:T(8,128)S(1)}, f32[512,16]{0,1:T(8,128)S(1)}, u32[]{:S(2)}, u32[]{:S(2)}) collective-permute-start(f32[512,16]{0,1:T(8,128)S(1)} %multiply_add_fusion.3), channel_id=1, source_target_pairs={{0,16},{16,32},{32,48},{48,64},{64,80},{80,96},{96,112},{112,128},... | collective-permute-start | bytes 98312 | tf_op jit(solution)/shard_map/while/body/eval_jaxpr/ppermute | solution.py:16
  334.2 6.8 %collective-permute-start = (f32[512,16]{0,1:T(8,128)S(1)}, f32[512,16]{0,1:T(8,128)S(1)}, u32[]{:S(2)}, u32[]{:S(2)}) collective-permute-start(f32[512,16]{0,1:T(8,128)S(1)} %multiply_add_fusion.3), channel_id=1, source_target_pairs={{0,16},{16,32},{32,48},{48,64},{64,80},{80,96},{96,112},{112,128},... | collective-permute-start | bytes 98312 | tf_op jit(solution)/shard_map/while/body/eval_jaxpr/ppermute | solution.py:16
  340.9 6.8 %collective-permute-start = (f32[512,16]{0,1:T(8,128)S(1)}, f32[512,16]{0,1:T(8,128)S(1)}, u32[]{:S(2)}, u32[]{:S(2)}) collective-permute-start(f32[512,16]{0,1:T(8,128)S(1)} %multiply_add_fusion.3), channel_id=1, source_target_pairs={{0,16},{16,32},{32,48},{48,64},{64,80},{80,96},{96,112},{112,128},... | collective-permute-start | bytes 98312 | tf_op jit(solution)/shard_map/while/body/eval_jaxpr/ppermute | solution.py:16
  352.1 156.4 %all-gather.14.cloned.1.call-start = ((), (), s32[]{:S(2)}) async-start(), calls=%async_computation.9 | async-start | bytes 4456448 | tf_op jit(solution)/shard_map/all_gather | solution.py:137
  455.3 150.4 %reduce-scatter.5.cloned.1.call-start = ((), (), s32[]{:S(2)}) async-start(), calls=%async_computation.10 | async-start | bytes 4456448 | tf_op jit(solution)/shard_map/reduce_scatter | solution.py:146
  607.5 21.1 %all-to-all-start.1 = ((bf16[16,2,4096]{2,1,0:T(2,128)(2,1)}), bf16[16,2,4096]{2,1,0:T(2,128)(2,1)S(1)}, u32[]{:S(2)}, u32[]{:S(2)}) async-start(bf16[16,2,4096]{2,1,0:T(2,128)(2,1)} %reshape.76), calls=%async_computation.3 | async-start | bytes 524288 | tf_op jit(solution)/shard_map/all_to_all | solution.py:149
  (7 other events, 1065.3 us)
Sparse Core Ops, SparseCore 0:
  9.1 41.8 all-gather.5
  53.4 55.2 all-gather.7
  111.1 56.2 all-gather.9
  169.7 61.4 all-gather.11
  352.2 81.6 reduce-scatter.2
  455.4 53.0 all-gather.13
  524.8 80.7 reduce-scatter.4
where the time goes:
time: 637 us; the launch traced here: 636 us
  waiting for transfers between devices  394 us (62%)
  starting transfers between devices  87.9 us (14%)
  matrix products  67.4 us (11%)
  blocking collectives  65.7 us (10%)
  between operations  13.7 us (2%)
    reduce_scatter x1, waiting for transfers between devices, local(): lax.psum_scatter(jnp.dot(blender_result, out_whole, preferred_element_typ...  81 us
    reduce_scatter x1, waiting for transfers between devices, local(): lax.psum_scatter(partial_out.astype(jnp.bfloat16), 'ctx', scatter_dimensi...  81 us
    ppermute x16, starting transfers between devices, shifted(): return lax.ppermute(shard, axis, pairs)  78.2 us
    all_gather x1, waiting for transfers between devices, local(): lax.all_gather(input_weight, 'ctx', axis=0, tiled=True)  57.7 us
    all_gather x1, waiting for transfers between devices, local(): shard_rows = lax.all_gather(arrived, 'ctx', axis=0, tiled=True)  53 us
    all_gather x1, waiting for transfers between devices, local(): lax.all_gather(gate_weight, 'ctx', axis=0, tiled=True)  52.4 us
    psum x1, blocking collectives, local(): lax.psum(jnp.dot(mixer_in, state_weight, preferred_element_type=jnp.float...  46.7 us
    all_gather x1, waiting for transfers between devices, local(): whole_stretch = lax.all_gather(tokens, 'exp', axis=1, tiled=True)  39.5 us
  transfers between devices with their start and end apart: 24, of which 22 were waited for; matrix products, arithmetic and copies ran while one was open for 8% of the time, Pallas kernels for 0%

commit v1 on v0

--- a/solution.py
+++ b/solution.py
@@ -8,6 +8,22 @@
 TOP = 2
 CAP = 2
 precise = lax.Precision.HIGHEST
+
+
+def gather_around(x, axis, dim):
+    ways, here, step = (lax.axis_size(axis), lax.axis_index(axis), x.shape[dim])
+    dims = [n * ways if d == dim else n for d, n in enumerate(x.shape)]
+    full = lax.dynamic_update_slice_in_dim(jnp.zeros(dims, x.dtype), x, here * step, axis=dim)
+    going_up = going_down = x
+    for far in range(1, ways // 2 + 1):
+        going_up = lax.ppermute(going_up, axis, [(d, (d + 1) % ways) for d in range(ways)])
+        full = lax.dynamic_update_slice_in_dim(full, going_up, (here - far) % ways * step, axis=dim)
+        if 2 * far < ways:
+            going_down = lax.ppermute(going_down, axis, [(d, (d - 1) % ways) for d in range(ways)])
+            full = lax.dynamic_update_slice_in_dim(
+                full, going_down, (here + far) % ways * step, axis=dim
+            )
+    return full
 
 
 def shifted(shard, axis, by):
@@ -50,9 +66,7 @@
         preferred_element_type=jnp.float32,
     )
     inner_z = jnp.dot(
-        whole_stretch,
-        lax.all_gather(gate_weight, "ctx", axis=0, tiled=True),
-        preferred_element_type=jnp.float32,
+        whole_stretch, gather_around(gate_weight, "ctx", 0), preferred_element_type=jnp.float32
     )
     inner_x = inner_x.astype(jnp.bfloat16)
     inner_z = inner_z.astype(jnp.bfloat16)

time: 637 us -> 592 us (0.929)
  waiting for transfers between devices: 394 us -> 297 us
  starting transfers between devices: 87.9 us -> 124 us
  local copies, waits for them, and re-layouts: 4.31 us -> 18.1 us
    all_gather x1 -> x0, waiting for transfers between devices: 52.4 us -> none  [local(): lax.all_gather(gate_weight, 'ctx', axis=0, tiled=True)]
    all_gather x1, waiting for transfers between devices: 39.5 us -> 0.01 us  [local(): whole_stretch = lax.all_gather(tokens, 'exp', axis=1, tiled=True)]
    ppermute x0 -> x15, starting transfers between devices: none -> 36 us  [the longest x7 33.8 us: gather_around(): lax.ppermute(going_down, axis, [(d, (d - 1) % ways) for d in range(ways)])]
    all_gather x1, waiting for transfers between devices: 57.7 us -> 26.7 us  [local(): lax.all_gather(input_weight, 'ctx', axis=0, tiled=True)]
    ppermute x0 -> x15, waiting for transfers between devices: none -> 26.4 us  [the longest x8 17 us: gather_around(): lax.ppermute(going_up, axis, [(d, (d + 1) % ways) for d in range(ways)])]
    dynamic_update_slice x0 -> x16, local copies, waits for them, and re-layouts: none -> 11.6 us  [the longest x8 5.77 us: gather_around(): lax.dynamic_update_slice_in_dim(full, going_up, (here - far) % ways * ste...]
  transfers between devices with their start and end apart: 24 -> 38, of which waited for: 22 -> 30; matrix products, arithmetic and copies ran while one was open for 8% -> 11% of each run, Pallas kernels for 0% -> 0%
where the time goes in v1:
time: 592 us; the launch traced here: 591 us
  waiting for transfers between devices  297 us (50%)
  starting transfers between devices  124 us (21%)
  matrix products  67.6 us (11%)
  blocking collectives  66.8 us (11%)
  local copies, waits for them, and re-layouts  18.1 us (3%)
  between operations  13.7 us (2%)
    reduce_scatter x1, waiting for transfers between devices, local(): lax.psum_scatter(jnp.dot(blender_result, out_whole, preferred_element_typ...  82.1 us
    reduce_scatter x1, waiting for transfers between devices, local(): lax.psum_scatter(partial_out.astype(jnp.bfloat16), 'ctx', scatter_dimensi...  80.9 us
    ppermute x16, starting transfers between devices, shifted(): return lax.ppermute(shard, axis, pairs)  78.2 us
    all_gather x1, waiting for transfers between devices, local(): shard_rows = lax.all_gather(arrived, 'ctx', axis=0, tiled=True)  52.9 us
    psum x1, blocking collectives, local(): lax.psum(jnp.dot(mixer_in, state_weight, preferred_element_type=jnp.float...  47.4 us
    dot_general x4, matrix products, causal_part(): jnp.einsum('ts,tsc,sc->tc', scores, weight, input_block, precision=precise)  38.7 us
    ppermute x7, starting transfers between devices, gather_around(): lax.ppermute(going_down, axis, [(d, (d - 1) % ways) for d in range(ways)])  33.8 us
    all_gather x1, waiting for transfers between devices, local(): lax.all_gather(input_weight, 'ctx', axis=0, tiled=True)  26.7 us
  transfers between devices with their start and end apart: 38, of which 30 were waited for; matrix products, arithmetic and copies ran while one was open for 11% of the time, Pallas kernels for 0%

profile of v1, /device:TPU:1, one launch (start us, length us, event | category | flops | bytes accessed | tf_op | source)
XLA Modules:
  0.0 590.6 jit_solution(14906479348774006445)
XLA Ops:
  86.4 26.7 %all-gather.7.cloned.1.call-done = bf16[4096,512]{1,0:T(8,128)(2,1)} async-done(((bf16[256,512]{1,0:T(8,128)(2,1)}), bf16[4096,512]{1,0:T(8,128)(2,1)}) %all-gather.7.cloned.1.call-update) | async-done | bytes 4194320 | tf_op jit(solution)/shard_map/all_gather | solution.py:65
  122.8 47.4 %psum.7 = f32[128,32]{0,1:T(8,128)S(1)} all-reduce(f32[128,32]{0,1:T(8,128)S(1)} %fusion.55), channel_id=1, replica_groups=mesh['ctx'=16,'exp'=16] {'exp'}, use_global_device_ids=true, to_apply=%region_1.2 | all-reduce | flops 4096 | bytes 32768 | tf_op jit(solution)/shard_map/psum | solution.py:82
  170.9 39.0 %while.20 = (s32[]{:T(128)}, f32[4,128,128]{2,1,0:T(8,128)S(1)}, f32[4,128,128]{2,1,0:T(8,128)S(1)}, f32[4,128,128]{2,1,0:T(8,128)S(1)}, f32[128,128]{1,0:T(8,128)S(1)}, /*index=5*/s32[]{:T(128)}) while((s32[]{:T(128)}, f32[4,128,128]{2,1,0:T(8,128)S(1)}, f32[4,128,128]{2,1,0:T(8,128)S(1)}, f32[4,128,128]{2,1,0:T(8,128)S(1)}, ...), condition=%wide.region_3.4_spmd, body=%wide.region_2.3_spmd.sunk | while | flops 35667968 | bytes 688205 | solution.py:93
  170.9 9.7 %fusion.88 = f32[128,1,128]{2,1,0:T(1,128)S(1)} fusion(f32[128,128,1]{1,2,0:T(1,128)S(1)} %bitcast.90, f32[128,128]{1,0:T(8,128)S(1)} %get-tuple-element.140, f32[128,128]{1,0:T(8,128)S(1)} %get-tuple-element.141, pred[128,128]{1,0:T(8,128)(4,1)S(1)} %iota_compare_fusion.5), kind=kOutput, calls=%fused_computation.clone.1 | convolution fusion | flops 35651584 | bytes 278528 | tf_op jit(solution)/shard_map/while/body/eval_jaxpr/ts,tsc,sc->tc/dot_general | solution.py:40
  180.7 9.7 %fusion.88 = f32[128,1,128]{2,1,0:T(1,128)S(1)} fusion(f32[128,128,1]{1,2,0:T(1,128)S(1)} %bitcast.90, f32[128,128]{1,0:T(8,128)S(1)} %get-tuple-element.140, f32[128,128]{1,0:T(8,128)S(1)} %get-tuple-element.141, pred[128,128]{1,0:T(8,128)(4,1)S(1)} %iota_compare_fusion.5), kind=kOutput, calls=%fused_computation.clone.1 | convolution fusion | flops 35651584 | bytes 278528 | tf_op jit(solution)/shard_map/while/body/eval_jaxpr/ts,tsc,sc->tc/dot_general | solution.py:40
  190.5 9.7 %fusion.88 = f32[128,1,128]{2,1,0:T(1,128)S(1)} fusion(f32[128,128,1]{1,2,0:T(1,128)S(1)} %bitcast.90, f32[128,128]{1,0:T(8,128)S(1)} %get-tuple-element.140, f32[128,128]{1,0:T(8,128)S(1)} %get-tuple-element.141, pred[128,128]{1,0:T(8,128)(4,1)S(1)} %iota_compare_fusion.5), kind=kOutput, calls=%fused_computation.clone.1 | convolution fusion | flops 35651584 | bytes 278528 | tf_op jit(solution)/shard_map/while/body/eval_jaxpr/ts,tsc,sc->tc/dot_general | solution.py:40
  200.2 9.7 %fusion.88 = f32[128,1,128]{2,1,0:T(1,128)S(1)} fusion(f32[128,128,1]{1,2,0:T(1,128)S(1)} %bitcast.90, f32[128,128]{1,0:T(8,128)S(1)} %get-tuple-element.140, f32[128,128]{1,0:T(8,128)S(1)} %get-tuple-element.141, pred[128,128]{1,0:T(8,128)(4,1)S(1)} %iota_compare_fusion.5), kind=kOutput, calls=%fused_computation.clone.1 | convolution fusion | flops 35651584 | bytes 278528 | tf_op jit(solution)/shard_map/while/body/eval_jaxpr/ts,tsc,sc->tc/dot_general | solution.py:40
  209.9 90.5 %while.21 = (s32[]{:T(128)}, f32[512,16]{0,1:T(8,128)S(1)}, f32[512]{0:T(512)S(1)}, f32[512,16]{0,1:T(8,128)S(1)}, s32[]{:T(128)}) while((s32[]{:T(128)}, f32[512,16]{0,1:T(8,128)S(1)}, f32[512]{0:T(512)S(1)}, f32[512,16]{0,1:T(8,128)S(1)}, s32[]{:T(128)}) %tuple.40), condition=%wide.region_5.6_spmd, body=%wide.region_4.5_spmd.sunk | while | flops 16386 | bytes 231525 | solution.py:106
  231.9 5.8 collective-permute-start
  238.7 5.9 %collective-permute-start = (f32[512,16]{0,1:T(8,128)S(1)}, f32[512,16]{0,1:T(8,128)S(1)}, u32[]{:S(2)}, u32[]{:S(2)}) collective-permute-start(f32[512,16]{0,1:T(8,128)S(1)} %multiply_add_fusion.3), channel_id=1, source_target_pairs={{0,16},{16,32},{32,48},{48,64},{64,80},{80,96},{96,112},{112,128},... | collective-permute-start | bytes 98312 | tf_op jit(solution)/shard_map/while/body/eval_jaxpr/ppermute | solution.py:32
  245.6 6.1 %collective-permute-start = (f32[512,16]{0,1:T(8,128)S(1)}, f32[512,16]{0,1:T(8,128)S(1)}, u32[]{:S(2)}, u32[]{:S(2)}) collective-permute-start(f32[512,16]{0,1:T(8,128)S(1)} %multiply_add_fusion.3), channel_id=1, source_target_pairs={{0,16},{16,32},{32,48},{48,64},{64,80},{80,96},{96,112},{112,128},... | collective-permute-start | bytes 98312 | tf_op jit(solution)/shard_map/while/body/eval_jaxpr/ppermute | solution.py:32
  252.7 5.8 collective-permute-start
  259.5 5.8 collective-permute-start
  266.3 5.8 collective-permute-start
  273.1 5.8 collective-permute-start
  286.6 5.8 collective-permute-start
  293.4 6.0 %collective-permute-start = (f32[512,16]{0,1:T(8,128)S(1)}, f32[512,16]{0,1:T(8,128)S(1)}, u32[]{:S(2)}, u32[]{:S(2)}) collective-permute-start(f32[512,16]{0,1:T(8,128)S(1)} %multiply_add_fusion.3), channel_id=1, source_target_pairs={{0,16},{16,32},{32,48},{48,64},{64,80},{80,96},{96,112},{112,128},... | collective-permute-start | bytes 98312 | tf_op jit(solution)/shard_map/while/body/eval_jaxpr/ppermute | solution.py:32
  305.7 82.1 %reduce-scatter.3.cloned.1.call-done = bf16[8,4096]{1,0:T(8,128)(2,1)} async-done(((bf16[128,4096]{1,0:T(8,128)(2,1)}), bf16[8,4096]{1,0:T(8,128)(2,1)}) %reduce-scatter.3.cloned.1.call-update) | async-done | bytes 65552 | tf_op jit(solution)/shard_map/reduce_scatter | solution.py:116
  389.3 19.4 %all_to_all.10 = bf16[16,2,4096]{2,1,0:T(2,128)(2,1)S(1)} all-to-all(bf16[16,2,4096]{2,1,0:T(2,128)(2,1)S(1)} %reshape.74), channel_id=1, replica_groups=mesh['ctx'=16,'exp'=16] {'exp'}, dimensions={0} | all-to-all | bytes 524288 | tf_op jit(solution)/shard_map/all_to_all | solution.py:146
  409.8 52.9 %all-gather.11.cloned.1.call-done = bf16[512,4096]{1,0:T(8,128)(2,1)} async-done(((bf16[32,4096]{1,0:T(8,128)(2,1)}), bf16[512,4096]{1,0:T(8,128)(2,1)}) %all-gather.11.cloned.1.call-update) | async-done | bytes 4194320 | tf_op jit(solution)/shard_map/all_gather | solution.py:151
  468.2 10.8 %convolution_convert_fusion = bf16[512,4096]{1,0:T(8,128)(2,1)} fusion(bf16[1,448,4096]{2,1,0:T(8,128)(2,1)} %param.32, bf16[512,4096]{1,0:T(8,128)(2,1)} %all-gather.11.cloned.1.call-done, bf16[1,448,4096]{2,1,0:T(8,128)(2,1)} %param.31, f32[512,448]{0,1:T(8,128)S(1)} %fusion.18), kind=kOutput, calls=%fused_computation.19 | convolution fusion | flops 3761569792 | bytes 16646144 | tf_op jit(solution)/shard_map/dot_general | solution.py:159
  479.0 80.9 %reduce-scatter.5.cloned.1.call-done = bf16[32,4096]{1,0:T(8,128)(2,1)} async-done(((bf16[512,4096]{1,0:T(8,128)(2,1)}), bf16[32,4096]{1,0:T(8,128)(2,1)}) %reduce-scatter.5.cloned.1.call-update) | async-done | bytes 262160 | tf_op jit(solution)/shard_map/reduce_scatter | solution.py:160
  561.7 9.3 %all-to-all-start.1 = ((bf16[16,2,4096]{2,1,0:T(2,128)(2,1)}), bf16[16,2,4096]{2,1,0:T(2,128)(2,1)S(1)}, u32[]{:S(2)}, u32[]{:S(2)}) async-start(bf16[16,2,4096]{2,1,0:T(2,128)(2,1)} %reshape.76), calls=%async_computation.3 | async-start | bytes 524288 | tf_op jit(solution)/shard_map/all_to_all | solution.py:163
  571.6 11.2 %all-to-all-done.1 = bf16[16,2,4096]{2,1,0:T(2,128)(2,1)S(1)} async-done(((bf16[16,2,4096]{2,1,0:T(2,128)(2,1)}), bf16[16,2,4096]{2,1,0:T(2,128)(2,1)S(1)}, u32[]{:S(2)}, u32[]{:S(2)}) %all-to-all-start.1) | async-done | bytes 262176 | tf_op jit(solution)/shard_map/all_to_all | solution.py:163
  (167 shorter events, 144.5 us)
Async XLA Ops:
  6.5 79.9 %all-gather.5.cloned.1.call-start = ((), (), s32[]{:S(2)}) async-start(), calls=%async_computation.4 | async-start | bytes 1114112 | tf_op jit(solution)/shard_map/all_gather | solution.py:60
  7.3 105.8 %all-gather.7.cloned.1.call-start = ((), (), s32[]{:S(2)}) async-start(), calls=%async_computation.5 | async-start | bytes 4456448 | tf_op jit(solution)/shard_map/all_gather | solution.py:65
  8.0 293.0 %all-gather.9.cloned.1.call-start = ((), (), s32[]{:S(2)}) async-start(), calls=%async_computation.6 | async-start | bytes 4456448 | tf_op jit(solution)/shard_map/all_gather | solution.py:115
  8.1 10.1 %collective-permute-start.2 = (bf16[256,512]{1,0:T(8,128)(2,1)}, bf16[256,512]{1,0:T(8,128)(2,1)S(1)}, u32[]{:S(2)}, u32[]{:S(2)}) collective-permute-start(bf16[256,512]{1,0:T(8,128)(2,1)} %param.21), channel_id=1, source_target_pairs={{0,16},{16,32},{32,48},{48,64},{64,80},{80,96},{96,112},{112,128},... | collective-permute-start | bytes 786440 | tf_op jit(solution)/shard_map/ppermute | solution.py:19
  10.2 8.0 %collective-permute-start.3 = (bf16[256,512]{1,0:T(8,128)(2,1)}, bf16[256,512]{1,0:T(8,128)(2,1)S(1)}, u32[]{:S(2)}, u32[]{:S(2)}) collective-permute-start(bf16[256,512]{1,0:T(8,128)(2,1)} %param.21), channel_id=1, source_target_pairs={{0,240},{16,0},{32,16},{48,32},{64,48},{80,64},{96,80},{112,96},{1... | collective-permute-start | bytes 786440 | tf_op jit(solution)/shard_map/ppermute | solution.py:22
  18.2 8.5 %collective-permute-start.4 = (bf16[256,512]{1,0:T(8,128)(2,1)S(1)}, bf16[256,512]{1,0:T(8,128)(2,1)S(1)}, u32[]{:S(2)}, u32[]{:S(2)}) collective-permute-start(bf16[256,512]{1,0:T(8,128)(2,1)S(1)} %collective-permute-done.2), channel_id=1, source_target_pairs={{0,16},{16,32},{32,48},{48,64},{64,80},{80,96},{96,112},{112,128},... | collective-permute-start | bytes 786440 | tf_op jit(solution)/shard_map/ppermute | solution.py:19
  18.2 10.6 %collective-permute-start.5 = (bf16[256,512]{1,0:T(8,128)(2,1)S(1)}, bf16[256,512]{1,0:T(8,128)(2,1)S(1)}, u32[]{:S(2)}, u32[]{:S(2)}) collective-permute-start(bf16[256,512]{1,0:T(8,128)(2,1)S(1)} %collective-permute-done.3), channel_id=1, source_target_pairs={{0,240},{16,0},{32,16},{48,32},{64,48},{80,64},{96,80},{112,96},{1... | collective-permute-start | bytes 786440 | tf_op jit(solution)/shard_map/ppermute | solution.py:22
  23.0 364.8 %reduce-scatter.3.cloned.1.call-start = ((), (), s32[]{:S(2)}) async-start(), calls=%async_computation.7 | async-start | bytes 1114112 | tf_op jit(solution)/shard_map/reduce_scatter | solution.py:116
  26.7 8.5 %collective-permute-start.6 = (bf16[256,512]{1,0:T(8,128)(2,1)S(1)}, bf16[256,512]{1,0:T(8,128)(2,1)S(1)}, u32[]{:S(2)}, u32[]{:S(2)}) collective-permute-start(bf16[256,512]{1,0:T(8,128)(2,1)S(1)} %collective-permute-done.4), channel_id=1, source_target_pairs={{0,16},{16,32},{32,48},{48,64},{64,80},{80,96},{96,112},{112,128},... | collective-permute-start | bytes 786440 | tf_op jit(solution)/shard_map/ppermute | solution.py:19
  28.8 10.2 %collective-permute-start.7 = (bf16[256,512]{1,0:T(8,128)(2,1)S(1)}, bf16[256,512]{1,0:T(8,128)(2,1)S(1)}, u32[]{:S(2)}, u32[]{:S(2)}) collective-permute-start(bf16[256,512]{1,0:T(8,128)(2,1)S(1)} %collective-permute-done.5), channel_id=1, source_target_pairs={{0,240},{16,0},{32,16},{48,32},{64,48},{80,64},{96,80},{112,96},{1... | collective-permute-start | bytes 786440 | tf_op jit(solution)/shard_map/ppermute | solution.py:22
  35.3 9.2 %collective-permute-start.8 = (bf16[256,512]{1,0:T(8,128)(2,1)S(1)}, bf16[256,512]{1,0:T(8,128)(2,1)S(1)}, u32[]{:S(2)}, u32[]{:S(2)}) collective-permute-start(bf16[256,512]{1,0:T(8,128)(2,1)S(1)} %collective-permute-done.6), channel_id=1, source_target_pairs={{0,16},{16,32},{32,48},{48,64},{64,80},{80,96},{96,112},{112,128},... | collective-permute-start | bytes 786440 | tf_op jit(solution)/shard_map/ppermute | solution.py:19
  39.0 8.1 %collective-permute-start.9 = (bf16[256,512]{1,0:T(8,128)(2,1)S(1)}, bf16[256,512]{1,0:T(8,128)(2,1)S(1)}, u32[]{:S(2)}, u32[]{:S(2)}) collective-permute-start(bf16[256,512]{1,0:T(8,128)(2,1)S(1)} %collective-permute-done.7), channel_id=1, source_target_pairs={{0,240},{16,0},{32,16},{48,32},{64,48},{80,64},{96,80},{112,96},{1... | collective-permute-start | bytes 786440 | tf_op jit(solution)/shard_map/ppermute | solution.py:22
  44.5 8.5 %collective-permute-start.10 = (bf16[256,512]{1,0:T(8,128)(2,1)S(1)}, bf16[256,512]{1,0:T(8,128)(2,1)S(1)}, u32[]{:S(2)}, u32[]{:S(2)}) collective-permute-start(bf16[256,512]{1,0:T(8,128)(2,1)S(1)} %collective-permute-done.8), channel_id=1, source_target_pairs={{0,16},{16,32},{32,48},{48,64},{64,80},{80,96},{96,112},{112,128},... | collective-permute-start | bytes 786440 | tf_op jit(solution)/shard_map/ppermute | solution.py:19
  47.1 9.0 %collective-permute-start.11 = (bf16[256,512]{1,0:T(8,128)(2,1)S(1)}, bf16[256,512]{1,0:T(8,128)(2,1)S(1)}, u32[]{:S(2)}, u32[]{:S(2)}) collective-permute-start(bf16[256,512]{1,0:T(8,128)(2,1)S(1)} %collective-permute-done.9), channel_id=1, source_target_pairs={{0,240},{16,0},{32,16},{48,32},{64,48},{80,64},{96,80},{112,96},{1... | collective-permute-start | bytes 786440 | tf_op jit(solution)/shard_map/ppermute | solution.py:22
  53.0 9.3 %collective-permute-start.12 = (bf16[256,512]{1,0:T(8,128)(2,1)S(1)}, bf16[256,512]{1,0:T(8,128)(2,1)S(1)}, u32[]{:S(2)}, u32[]{:S(2)}) collective-permute-start(bf16[256,512]{1,0:T(8,128)(2,1)S(1)} %collective-permute-done.10), channel_id=1, source_target_pairs={{0,16},{16,32},{32,48},{48,64},{64,80},{80,96},{96,112},{112,128},... | collective-permute-start | bytes 786440 | tf_op jit(solution)/shard_map/ppermute | solution.py:19
  56.1 11.4 %collective-permute-start.13 = (bf16[256,512]{1,0:T(8,128)(2,1)S(1)}, bf16[256,512]{1,0:T(8,128)(2,1)S(1)}, u32[]{:S(2)}, u32[]{:S(2)}) collective-permute-start(bf16[256,512]{1,0:T(8,128)(2,1)S(1)} %collective-permute-done.11), channel_id=1, source_target_pairs={{0,240},{16,0},{32,16},{48,32},{64,48},{80,64},{96,80},{112,96},{1... | collective-permute-start | bytes 786440 | tf_op jit(solution)/shard_map/ppermute | solution.py:22
  62.4 13.1 %collective-permute-start.14 = (bf16[256,512]{1,0:T(8,128)(2,1)S(1)}, bf16[256,512]{1,0:T(8,128)(2,1)S(1)}, u32[]{:S(2)}, u32[]{:S(2)}) collective-permute-start(bf16[256,512]{1,0:T(8,128)(2,1)S(1)} %collective-permute-done.12), channel_id=1, source_target_pairs={{0,16},{16,32},{32,48},{48,64},{64,80},{80,96},{96,112},{112,128},... | collective-permute-start | bytes 786440 | tf_op jit(solution)/shard_map/ppermute | solution.py:19
  67.5 12.4 %collective-permute-start.15 = (bf16[256,512]{1,0:T(8,128)(2,1)S(1)}, bf16[256,512]{1,0:T(8,128)(2,1)S(1)}, u32[]{:S(2)}, u32[]{:S(2)}) collective-permute-start(bf16[256,512]{1,0:T(8,128)(2,1)S(1)} %collective-permute-done.13), channel_id=1, source_target_pairs={{0,240},{16,0},{32,16},{48,32},{64,48},{80,64},{96,80},{112,96},{1... | collective-permute-start | bytes 786440 | tf_op jit(solution)/shard_map/ppermute | solution.py:22
  75.5 10.2 %collective-permute-start.16 = (bf16[256,512]{1,0:T(8,128)(2,1)S(1)}, bf16[256,512]{1,0:T(8,128)(2,1)S(1)}, u32[]{:S(2)}, u32[]{:S(2)}) collective-permute-start(bf16[256,512]{1,0:T(8,128)(2,1)S(1)} %collective-permute-done.14), channel_id=1, source_target_pairs={{0,16},{16,32},{32,48},{48,64},{64,80},{80,96},{96,112},{112,128},... | collective-permute-start | bytes 786440 | tf_op jit(solution)/shard_map/ppermute | solution.py:19
  245.6 7.1 %collective-permute-start = (f32[512,16]{0,1:T(8,128)S(1)}, f32[512,16]{0,1:T(8,128)S(1)}, u32[]{:S(2)}, u32[]{:S(2)}) collective-permute-start(f32[512,16]{0,1:T(8,128)S(1)} %multiply_add_fusion.3), channel_id=1, source_target_pairs={{0,16},{16,32},{32,48},{48,64},{64,80},{80,96},{96,112},{112,128},... | collective-permute-start | bytes 98312 | tf_op jit(solution)/shard_map/while/body/eval_jaxpr/ppermute | solution.py:32
  293.4 7.1 %collective-permute-start = (f32[512,16]{0,1:T(8,128)S(1)}, f32[512,16]{0,1:T(8,128)S(1)}, u32[]{:S(2)}, u32[]{:S(2)}) collective-permute-start(f32[512,16]{0,1:T(8,128)S(1)} %multiply_add_fusion.3), channel_id=1, source_target_pairs={{0,16},{16,32},{32,48},{48,64},{64,80},{80,96},{96,112},{112,128},... | collective-permute-start | bytes 98312 | tf_op jit(solution)/shard_map/while/body/eval_jaxpr/ppermute | solution.py:32
  305.0 157.8 %all-gather.11.cloned.1.call-start = ((), (), s32[]{:S(2)}) async-start(), calls=%async_computation.8 | async-start | bytes 4456448 | tf_op jit(solution)/shard_map/all_gather | solution.py:151
  409.5 150.3 %reduce-scatter.5.cloned.1.call-start = ((), (), s32[]{:S(2)}) async-start(), calls=%async_computation.9 | async-start | bytes 4456448 | tf_op jit(solution)/shard_map/reduce_scatter | solution.py:160
  561.7 21.1 %all-to-all-start.1 = ((bf16[16,2,4096]{2,1,0:T(2,128)(2,1)}), bf16[16,2,4096]{2,1,0:T(2,128)(2,1)S(1)}, u32[]{:S(2)}, u32[]{:S(2)}) async-start(bf16[16,2,4096]{2,1,0:T(2,128)(2,1)} %reshape.76), calls=%async_computation.3 | async-start | bytes 524288 | tf_op jit(solution)/shard_map/all_to_all | solution.py:163
  (22 other events, 946.0 us)
Sparse Core Ops, SparseCore 0:
  9.1 41.7 all-gather.4
  53.4 59.6 all-gather.6
  115.5 61.4 all-gather.8
  305.1 82.7 reduce-scatter.2
  409.7 53.0 all-gather.10
  479.1 80.7 reduce-scatter.4
